TPU v7x, 512 devices: a whole 4x4x16 slice. The times are simulated.
512 devices in a mesh: req: 16 (over z), ctx: 32 (over x, y, core).
Axes of the slice: x: 4, y: 4, z: 16, core: 2. Of those that a mesh axis runs over, the one named last changes fastest.
Arguments:
- query_rows: bfloat16 [131072, 1024], P(('req', 'ctx')), parts along dimension 0, may hold values from -8 to 8
- key_rows: bfloat16 [131072, 128], P(('req', 'ctx')), parts along dimension 0, may hold values from -8 to 8
- value_rows: bfloat16 [131072, 128], P(('req', 'ctx')), parts along dimension 0, may hold values from -8 to 8
- document_ids: int32 [131072], P('req'), parts along dimension 0, may hold values from 0 to 7, never falling along the last dimension, each value on 1 to 4096 neighbouring positions
Outputs:
- attended: bfloat16 [131072, 1024], P(('req', 'ctx')), parts along dimension 0
There are 16 independent parts, one for each index of `req`. A program takes and returns all parts, laid end to end along the dimension named above; each array names one. Nothing has to cross between parts.
All inputs are finite; a program needn't handle non-finite values.
Results may differ from a plain program's by a relative error of at most 0.004.
Values may be sent and summed in bfloat16 or wider, within the bound.
No kernel may reach another device: no remote copies, remote signals or barrier semaphores. Data moves between devices by JAX's collectives and lax.ppermute only.
A program may use at most 64 MiB of HBM per device.

v0:
```python
import math
import jax
import jax.numpy as jnp
from jax import lax
from jax.sharding import PartitionSpec as P


def make_absorb(stacked, positions, query_docs, document_ids):
    dim_size = stacked.shape[2]
    factor = 1.0 / math.sqrt(dim_size)

    def absorb(carry, piece, start, valid):
        key_piece, value_piece = piece
        length = key_piece.shape[0]
        block = math.gcd(length, 512)

        def one_block(state, which):
            offset = which * block
            key_block = lax.dynamic_slice_in_dim(key_piece, offset, block, 0)
            value_block = lax.dynamic_slice_in_dim(value_piece, offset, block, 0)
            key_positions = offset + jnp.arange(block, dtype=jnp.int32)
            key_docs = lax.dynamic_slice_in_dim(document_ids, jnp.maximum(offset, 0), block, 0)
            allowed = (
                valid
                & (query_docs[:, None] == key_docs[None, :])
                & (key_positions[None, :] <= positions[:, None])
            )

            def compute(inner):
                running, totals, accum = inner
                scores = (
                    jnp.einsum(
                        "thd,sd->ths", stacked, key_block, preferred_element_type=jnp.float32
                    )
                    * factor
                )
                masked = jnp.where(allowed[:, None, :], scores, jnp.float32(-1e30))
                newest = jnp.maximum(running, jnp.max(masked, axis=-1))
                weights = jnp.where(
                    allowed[:, None, :], jnp.exp(masked - newest[..., None]), jnp.float32(0.0)
                )
                shrink = jnp.exp(running - newest)
                totals = totals * shrink + jnp.sum(weights, axis=-1)
                accum = accum * shrink[..., None] + jnp.einsum(
                    "ths,sd->thd",
                    weights.astype(jnp.bfloat16),
                    value_block,
                    preferred_element_type=jnp.float32,
                )
                return (newest, totals, accum)

            def unchanged(inner):
                return inner

            return (lax.cond(jnp.any(allowed), compute, unchanged, state), None)

        result, _ = lax.scan(one_block, carry, jnp.arange(length // block, dtype=jnp.int32))
        return result

    return absorb


def start_state(stacked):
    count, head_count, dim_size = stacked.shape
    return (
        jnp.full((count, head_count), -1e30, jnp.float32),
        jnp.zeros((count, head_count), jnp.float32),
        jnp.zeros((count, head_count, dim_size), jnp.float32),
    )


def finish(state):
    running, totals, accum = state
    result = accum / totals[..., None]
    count = result.shape[0]
    return result.reshape(count, result.shape[1] * result.shape[2]).astype(jnp.bfloat16)


def split_heads(active, dim_size):
    count = active.shape[0]
    return active.reshape(count, active.shape[1] // dim_size, dim_size)


def on_device(query_rows, key_rows, value_rows, document_ids):
    local_rows = query_rows.shape[0]
    dim_size = key_rows.shape[1]
    device = lax.axis_index("ctx")
    offsets = jnp.arange(local_rows, dtype=jnp.int32)
    own_positions = device * local_rows + offsets
    query_docs = jnp.take(document_ids, own_positions)
    stacked = split_heads(query_rows, dim_size)
    absorb = make_absorb(stacked, own_positions, query_docs, document_ids)
    start = jnp.int32(0)
    state = absorb(
        start_state(stacked),
        (
            lax.all_gather(key_rows, "ctx", axis=0, tiled=True),
            lax.all_gather(value_rows, "ctx", axis=0, tiled=True),
        ),
        start,
        start >= 0,
    )
    attended = finish(state)
    return attended


def solution(mesh):
    in_specs = (P(("req", "ctx"), None), P(("req", "ctx"), None), P(("req", "ctx"), None), P("req"))
    out_specs = P(("req", "ctx"), None)
    return jax.shard_map(
        on_device, mesh=mesh, in_specs=in_specs, out_specs=out_specs, check_vma=False
    )
```

profile of v0, /device:TPU:4, one launch (start us, length us, event | category | flops | bytes accessed | tf_op | source)
XLA Modules:
  0.0 247.9 jit_solution(16759929622175136257)
XLA Ops:
  9.6 2.0 gather_fusion
  11.6 61.7 %all-gather.3.cloned.1.call-done = bf16[8192,128]{1,0:T(8,128)(2,1)} async-done(((bf16[256,128]{1,0:T(8,128)(2,1)}), bf16[8192,128]{1,0:T(8,128)(2,1)}) %all-gather.3.cloned.1.call-update) | async-done | bytes 2097168 | tf_op jit(solution)/shard_map/all_gather | solution.py:97
  73.3 61.5 %all-gather.5.cloned.1.call-done = bf16[8192,128]{1,0:T(8,128)(2,1)} async-done(((bf16[256,128]{1,0:T(8,128)(2,1)}), bf16[8192,128]{1,0:T(8,128)(2,1)}) %all-gather.5.cloned.1.call-update) | async-done | bytes 2097168 | tf_op jit(solution)/shard_map/all_gather | solution.py:98
  134.8 105.0 %while.15 = (s32[]{:T(128)}, f32[256,8]{0,1:T(8,128)S(1)}, f32[256,8]{0,1:T(8,128)S(1)}, f32[256,8,128]{2,0,1:T(8,128)S(1)}, s32[256]{0:T(256)S(1)}, /*index=5*/...) while((s32[]{:T(128)}, f32[256,8]{0,1:T(8,128)S(1)}, ...), condition=%wide.region_6.7_spmd.clone, body=%wide.region_0.6_spmd.clone.sunk | while | flops 551555840 | bytes 16135525 | solution.py:57
  138.4 5.4 %conditional.3 = ((f32[256,8]{0,1:T(8,128)S(1)}, f32[256,8]{0,1:T(8,128)S(1)}, f32[256,8,128]{2,0,1:T(8,128)S(1)})) conditional(s32[]{:T(128)} %convert_element_type.27, (f32[256,8]{0,1:T(8,128)S(1)}, f32[256,8]{0,1:T(8,128)S(1)}, f32[256,8,128]{2,0,1:T(8,128)S(1)}) %tuple.45, (pred[256,512]{0,1:T(8,128)(4,1)S(1)}, s32[]{:T(128)}, ...), branch_computations={%region_2.2_spmd, %region_3.5_spmd} | conditional | flops 551030784 | bytes 15990858 | solution.py:55
  138.4 1.7 fusion.2
  141.2 2.6 %fusion.8 = f32[256,8,128]{2,0,1:T(8,128)S(1)} fusion(f32[512,256,8]{1,0,2:T(8,128)S(1)} %get-tuple-element.234, f32[256,8]{0,1:T(8,128)S(1)} %max.7, pred[256,512]{0,1:T(8,128)(4,1)S(1)} %get-tuple-element.142, f32[256,8,128]{2,0,1:T(8,128)S(1)} %get-tuple-element.147, f32[256,8]{0,1:T(8,128)S(1)} %get-tuple-element.230, ...), kind=kOutput, calls=%fused_computation.9 | convolution fusion | flops 274202624 | bytes 6569988 | tf_op jit(solution)/shard_map/while/body/eval_jaxpr/cond/branch_1_fun/ths,sd->thd/dot_general | solution.py:44
  147.3 5.4 %conditional.3 = ((f32[256,8]{0,1:T(8,128)S(1)}, f32[256,8]{0,1:T(8,128)S(1)}, f32[256,8,128]{2,0,1:T(8,128)S(1)})) conditional(s32[]{:T(128)} %convert_element_type.27, (f32[256,8]{0,1:T(8,128)S(1)}, f32[256,8]{0,1:T(8,128)S(1)}, f32[256,8,128]{2,0,1:T(8,128)S(1)}) %tuple.45, (pred[256,512]{0,1:T(8,128)(4,1)S(1)}, s32[]{:T(128)}, ...), branch_computations={%region_2.2_spmd, %region_3.5_spmd} | conditional | flops 551030784 | bytes 15990858 | solution.py:55
  147.3 1.7 fusion.2
  150.1 2.6 %fusion.8 = f32[256,8,128]{2,0,1:T(8,128)S(1)} fusion(f32[512,256,8]{1,0,2:T(8,128)S(1)} %get-tuple-element.234, f32[256,8]{0,1:T(8,128)S(1)} %max.7, pred[256,512]{0,1:T(8,128)(4,1)S(1)} %get-tuple-element.142, f32[256,8,128]{2,0,1:T(8,128)S(1)} %get-tuple-element.147, f32[256,8]{0,1:T(8,128)S(1)} %get-tuple-element.230, ...), kind=kOutput, calls=%fused_computation.9 | convolution fusion | flops 274202624 | bytes 6569988 | tf_op jit(solution)/shard_map/while/body/eval_jaxpr/cond/branch_1_fun/ths,sd->thd/dot_general | solution.py:44
  156.2 5.4 %conditional.3 = ((f32[256,8]{0,1:T(8,128)S(1)}, f32[256,8]{0,1:T(8,128)S(1)}, f32[256,8,128]{2,0,1:T(8,128)S(1)})) conditional(s32[]{:T(128)} %convert_element_type.27, (f32[256,8]{0,1:T(8,128)S(1)}, f32[256,8]{0,1:T(8,128)S(1)}, f32[256,8,128]{2,0,1:T(8,128)S(1)}) %tuple.45, (pred[256,512]{0,1:T(8,128)(4,1)S(1)}, s32[]{:T(128)}, ...), branch_computations={%region_2.2_spmd, %region_3.5_spmd} | conditional | flops 551030784 | bytes 15990858 | solution.py:55
  159.0 2.6 %fusion.8 = f32[256,8,128]{2,0,1:T(8,128)S(1)} fusion(f32[512,256,8]{1,0,2:T(8,128)S(1)} %get-tuple-element.234, f32[256,8]{0,1:T(8,128)S(1)} %max.7, pred[256,512]{0,1:T(8,128)(4,1)S(1)} %get-tuple-element.142, f32[256,8,128]{2,0,1:T(8,128)S(1)} %get-tuple-element.147, f32[256,8]{0,1:T(8,128)S(1)} %get-tuple-element.230, ...), kind=kOutput, calls=%fused_computation.9 | convolution fusion | flops 274202624 | bytes 6569988 | tf_op jit(solution)/shard_map/while/body/eval_jaxpr/cond/branch_1_fun/ths,sd->thd/dot_general | solution.py:44
  165.1 5.4 %conditional.3 = ((f32[256,8]{0,1:T(8,128)S(1)}, f32[256,8]{0,1:T(8,128)S(1)}, f32[256,8,128]{2,0,1:T(8,128)S(1)})) conditional(s32[]{:T(128)} %convert_element_type.27, (f32[256,8]{0,1:T(8,128)S(1)}, f32[256,8]{0,1:T(8,128)S(1)}, f32[256,8,128]{2,0,1:T(8,128)S(1)}) %tuple.45, (pred[256,512]{0,1:T(8,128)(4,1)S(1)}, s32[]{:T(128)}, ...), branch_computations={%region_2.2_spmd, %region_3.5_spmd} | conditional | flops 551030784 | bytes 15990858 | solution.py:55
  167.9 2.6 %fusion.8 = f32[256,8,128]{2,0,1:T(8,128)S(1)} fusion(f32[512,256,8]{1,0,2:T(8,128)S(1)} %get-tuple-element.234, f32[256,8]{0,1:T(8,128)S(1)} %max.7, pred[256,512]{0,1:T(8,128)(4,1)S(1)} %get-tuple-element.142, f32[256,8,128]{2,0,1:T(8,128)S(1)} %get-tuple-element.147, f32[256,8]{0,1:T(8,128)S(1)} %get-tuple-element.230, ...), kind=kOutput, calls=%fused_computation.9 | convolution fusion | flops 274202624 | bytes 6569988 | tf_op jit(solution)/shard_map/while/body/eval_jaxpr/cond/branch_1_fun/ths,sd->thd/dot_general | solution.py:44
  174.1 5.4 %conditional.3 = ((f32[256,8]{0,1:T(8,128)S(1)}, f32[256,8]{0,1:T(8,128)S(1)}, f32[256,8,128]{2,0,1:T(8,128)S(1)})) conditional(s32[]{:T(128)} %convert_element_type.27, (f32[256,8]{0,1:T(8,128)S(1)}, f32[256,8]{0,1:T(8,128)S(1)}, f32[256,8,128]{2,0,1:T(8,128)S(1)}) %tuple.45, (pred[256,512]{0,1:T(8,128)(4,1)S(1)}, s32[]{:T(128)}, ...), branch_computations={%region_2.2_spmd, %region_3.5_spmd} | conditional | flops 551030784 | bytes 15990858 | solution.py:55
  176.9 2.6 %fusion.8 = f32[256,8,128]{2,0,1:T(8,128)S(1)} fusion(f32[512,256,8]{1,0,2:T(8,128)S(1)} %get-tuple-element.234, f32[256,8]{0,1:T(8,128)S(1)} %max.7, pred[256,512]{0,1:T(8,128)(4,1)S(1)} %get-tuple-element.142, f32[256,8,128]{2,0,1:T(8,128)S(1)} %get-tuple-element.147, f32[256,8]{0,1:T(8,128)S(1)} %get-tuple-element.230, ...), kind=kOutput, calls=%fused_computation.9 | convolution fusion | flops 274202624 | bytes 6569988 | tf_op jit(solution)/shard_map/while/body/eval_jaxpr/cond/branch_1_fun/ths,sd->thd/dot_general | solution.py:44
  183.0 5.4 %conditional.3 = ((f32[256,8]{0,1:T(8,128)S(1)}, f32[256,8]{0,1:T(8,128)S(1)}, f32[256,8,128]{2,0,1:T(8,128)S(1)})) conditional(s32[]{:T(128)} %convert_element_type.27, (f32[256,8]{0,1:T(8,128)S(1)}, f32[256,8]{0,1:T(8,128)S(1)}, f32[256,8,128]{2,0,1:T(8,128)S(1)}) %tuple.45, (pred[256,512]{0,1:T(8,128)(4,1)S(1)}, s32[]{:T(128)}, ...), branch_computations={%region_2.2_spmd, %region_3.5_spmd} | conditional | flops 551030784 | bytes 15990858 | solution.py:55
  185.8 2.6 %fusion.8 = f32[256,8,128]{2,0,1:T(8,128)S(1)} fusion(f32[512,256,8]{1,0,2:T(8,128)S(1)} %get-tuple-element.234, f32[256,8]{0,1:T(8,128)S(1)} %max.7, pred[256,512]{0,1:T(8,128)(4,1)S(1)} %get-tuple-element.142, f32[256,8,128]{2,0,1:T(8,128)S(1)} %get-tuple-element.147, f32[256,8]{0,1:T(8,128)S(1)} %get-tuple-element.230, ...), kind=kOutput, calls=%fused_computation.9 | convolution fusion | flops 274202624 | bytes 6569988 | tf_op jit(solution)/shard_map/while/body/eval_jaxpr/cond/branch_1_fun/ths,sd->thd/dot_general | solution.py:44
  191.9 5.4 %conditional.3 = ((f32[256,8]{0,1:T(8,128)S(1)}, f32[256,8]{0,1:T(8,128)S(1)}, f32[256,8,128]{2,0,1:T(8,128)S(1)})) conditional(s32[]{:T(128)} %convert_element_type.27, (f32[256,8]{0,1:T(8,128)S(1)}, f32[256,8]{0,1:T(8,128)S(1)}, f32[256,8,128]{2,0,1:T(8,128)S(1)}) %tuple.45, (pred[256,512]{0,1:T(8,128)(4,1)S(1)}, s32[]{:T(128)}, ...), branch_computations={%region_2.2_spmd, %region_3.5_spmd} | conditional | flops 551030784 | bytes 15990858 | solution.py:55
  194.7 2.6 %fusion.8 = f32[256,8,128]{2,0,1:T(8,128)S(1)} fusion(f32[512,256,8]{1,0,2:T(8,128)S(1)} %get-tuple-element.234, f32[256,8]{0,1:T(8,128)S(1)} %max.7, pred[256,512]{0,1:T(8,128)(4,1)S(1)} %get-tuple-element.142, f32[256,8,128]{2,0,1:T(8,128)S(1)} %get-tuple-element.147, f32[256,8]{0,1:T(8,128)S(1)} %get-tuple-element.230, ...), kind=kOutput, calls=%fused_computation.9 | convolution fusion | flops 274202624 | bytes 6569988 | tf_op jit(solution)/shard_map/while/body/eval_jaxpr/cond/branch_1_fun/ths,sd->thd/dot_general | solution.py:44
  200.8 5.4 %conditional.3 = ((f32[256,8]{0,1:T(8,128)S(1)}, f32[256,8]{0,1:T(8,128)S(1)}, f32[256,8,128]{2,0,1:T(8,128)S(1)})) conditional(s32[]{:T(128)} %convert_element_type.27, (f32[256,8]{0,1:T(8,128)S(1)}, f32[256,8]{0,1:T(8,128)S(1)}, f32[256,8,128]{2,0,1:T(8,128)S(1)}) %tuple.45, (pred[256,512]{0,1:T(8,128)(4,1)S(1)}, s32[]{:T(128)}, ...), branch_computations={%region_2.2_spmd, %region_3.5_spmd} | conditional | flops 551030784 | bytes 15990858 | solution.py:55
  203.6 2.6 %fusion.8 = f32[256,8,128]{2,0,1:T(8,128)S(1)} fusion(f32[512,256,8]{1,0,2:T(8,128)S(1)} %get-tuple-element.234, f32[256,8]{0,1:T(8,128)S(1)} %max.7, pred[256,512]{0,1:T(8,128)(4,1)S(1)} %get-tuple-element.142, f32[256,8,128]{2,0,1:T(8,128)S(1)} %get-tuple-element.147, f32[256,8]{0,1:T(8,128)S(1)} %get-tuple-element.230, ...), kind=kOutput, calls=%fused_computation.9 | convolution fusion | flops 274202624 | bytes 6569988 | tf_op jit(solution)/shard_map/while/body/eval_jaxpr/cond/branch_1_fun/ths,sd->thd/dot_general | solution.py:44
  209.8 5.4 %conditional.3 = ((f32[256,8]{0,1:T(8,128)S(1)}, f32[256,8]{0,1:T(8,128)S(1)}, f32[256,8,128]{2,0,1:T(8,128)S(1)})) conditional(s32[]{:T(128)} %convert_element_type.27, (f32[256,8]{0,1:T(8,128)S(1)}, f32[256,8]{0,1:T(8,128)S(1)}, f32[256,8,128]{2,0,1:T(8,128)S(1)}) %tuple.45, (pred[256,512]{0,1:T(8,128)(4,1)S(1)}, s32[]{:T(128)}, ...), branch_computations={%region_2.2_spmd, %region_3.5_spmd} | conditional | flops 551030784 | bytes 15990858 | solution.py:55
  212.6 2.6 %fusion.8 = f32[256,8,128]{2,0,1:T(8,128)S(1)} fusion(f32[512,256,8]{1,0,2:T(8,128)S(1)} %get-tuple-element.234, f32[256,8]{0,1:T(8,128)S(1)} %max.7, pred[256,512]{0,1:T(8,128)(4,1)S(1)} %get-tuple-element.142, f32[256,8,128]{2,0,1:T(8,128)S(1)} %get-tuple-element.147, f32[256,8]{0,1:T(8,128)S(1)} %get-tuple-element.230, ...), kind=kOutput, calls=%fused_computation.9 | convolution fusion | flops 274202624 | bytes 6569988 | tf_op jit(solution)/shard_map/while/body/eval_jaxpr/cond/branch_1_fun/ths,sd->thd/dot_general | solution.py:44
  (144 shorter events, 61.6 us)
Async XLA Ops:
  6.5 66.7 %all-gather.3.cloned.1.call-start = ((), (), s32[]{:S(2)}) async-start(), calls=%async_computation | async-start | bytes 2162688 | tf_op jit(solution)/shard_map/all_gather | solution.py:97
  7.3 127.5 %all-gather.5.cloned.1.call-start = ((), (), s32[]{:S(2)}) async-start(), calls=%async_computation.1 | async-start | bytes 2162688 | tf_op jit(solution)/shard_map/all_gather | solution.py:98
Sparse Core Ops, SparseCore 0:
  10.5 62.7 all-gather.2
  76.4 58.3 all-gather.4
where the time goes:
time: 250 us; the launch traced here: 248 us
  waiting for transfers between devices  125 us (50%)
  matrix products  38.9 us (16%)
  local copies, waits for them, and re-layouts  25.9 us (10%)
  other arithmetic  24 us (10%)
  loops' own time  21 us (8%)
  between operations  13.4 us (5%)
    all_gather x1, waiting for transfers between devices, on_device(): lax.all_gather(key_rows, 'ctx', axis=0, tiled=True)  61.7 us
    all_gather x1, waiting for transfers between devices, on_device(): lax.all_gather(value_rows, 'ctx', axis=0, tiled=True)  61.5 us
    dot_general x9, matrix products, compute(): jnp.einsum('ths,sd->thd', weights.astype(jnp.bfloat16), value_block, pref...  23.3 us
    another operation x1, loops' own time, absorb(): lax.scan(one_block, carry, jnp.arange(length // block, dtype=jnp.int32))  20.3 us
    dot_general x9, matrix products, compute(): jnp.einsum('thd,sd->ths', stacked, key_block, preferred_element_type=jnp....  15.5 us
    reduce_or x16, other arithmetic, one_block(): return (lax.cond(jnp.any(allowed), compute, unchanged, state), None)  13.5 us
    dynamic_slice x16, local copies, waits for them, and re-layouts, one_block(): lax.dynamic_slice_in_dim(document_ids, jnp.maximum(offset, 0), block, 0)  12.5 us
    dynamic_slice x16, local copies, waits for them, and re-layouts, absorb(): lax.scan(one_block, carry, jnp.arange(length // block, dtype=jnp.int32))  9.88 us
  transfers between devices with their start and end apart: 2, of which 2 were waited for; matrix products, arithmetic and copies ran while one was open for 1% of the time, Pallas kernels for 0%

commit v1 on v0

--- a/solution.py
+++ b/solution.py
@@ -94,7 +94,9 @@
     state = absorb(
         start_state(stacked),
         (
-            lax.all_gather(key_rows, "ctx", axis=0, tiled=True),
+            jnp.concatenate(
+                lax.all_to_all(jnp.stack([key_rows] * lax.axis_size("ctx")), "ctx", 0, 0), axis=0
+            ),
             lax.all_gather(value_rows, "ctx", axis=0, tiled=True),
         ),
         start,

time: 250 us -> 182 us (0.73)
  waiting for transfers between devices: 125 us -> 57 us
  starting transfers between devices: 0.04 us -> 10.3 us
  local copies, waits for them, and re-layouts: 25.9 us -> 16.1 us
    all_gather x1 -> x0, waiting for transfers between devices: 61.7 us -> none  [on_device(): lax.all_gather(key_rows, 'ctx', axis=0, tiled=True)]
    all_gather x1, waiting for transfers between devices: 61.5 us -> 32.2 us  [on_device(): lax.all_gather(value_rows, 'ctx', axis=0, tiled=True)]
    all_to_all x0 -> x1, waiting for transfers between devices: none -> 24.1 us  [on_device(): lax.all_to_all(jnp.stack([key_rows] * lax.axis_size('ctx')), 'ctx', 0, 0)]
    dynamic_slice x16, local copies, waits for them, and re-layouts: 12.5 us -> 1.3 us  [one_block(): lax.dynamic_slice_in_dim(document_ids, jnp.maximum(offset, 0), block, 0)]
    all_to_all x0 -> x1, starting transfers between devices: none -> 10.3 us  [on_device(): lax.all_to_all(jnp.stack([key_rows] * lax.axis_size('ctx')), 'ctx', 0, 0)]
    another operation x0 -> x1, local copies, waits for them, and re-layouts: none -> 2.64 us  [on_device(): jnp.stack([key_rows] * lax.axis_size('ctx'))]
  transfers between devices with their start and end apart: 2 -> 2, of which waited for: 2 -> 2; matrix products, arithmetic and copies ran while one was open for 1% -> 3% of each run, Pallas kernels for 0% -> 0%
where the time goes in v1:
time: 182 us; the launch traced here: 181 us
  waiting for transfers between devices  57 us (31%)
  matrix products  38.9 us (21%)
  other arithmetic  24 us (13%)
  loops' own time  21 us (12%)
  local copies, waits for them, and re-layouts  16.1 us (9%)
  between operations  13.5 us (7%)
  starting transfers between devices  10.3 us (6%)
    all_gather x1, waiting for transfers between devices, on_device(): lax.all_gather(value_rows, 'ctx', axis=0, tiled=True)  32.2 us
    all_to_all x1, waiting for transfers between devices, on_device(): lax.all_to_all(jnp.stack([key_rows] * lax.axis_size('ctx')), 'ctx', 0, 0)  24.1 us
    dot_general x9, matrix products, compute(): jnp.einsum('ths,sd->thd', weights.astype(jnp.bfloat16), value_block, pref...  23.4 us
    another operation x1, loops' own time, absorb(): lax.scan(one_block, carry, jnp.arange(length // block, dtype=jnp.int32))  20.3 us
    dot_general x9, matrix products, compute(): jnp.einsum('thd,sd->ths', stacked, key_block, preferred_element_type=jnp....  15.6 us
    reduce_or x16, other arithmetic, one_block(): return (lax.cond(jnp.any(allowed), compute, unchanged, state), None)  13.5 us
    all_to_all x1, starting transfers between devices, on_device(): lax.all_to_all(jnp.stack([key_rows] * lax.axis_size('ctx')), 'ctx', 0, 0)  10.3 us
    dynamic_slice x16, local copies, waits for them, and re-layouts, absorb(): lax.scan(one_block, carry, jnp.arange(length // block, dtype=jnp.int32))  9.88 us
  transfers between devices with their start and end apart: 2, of which 2 were waited for; matrix products, arithmetic and copies ran while one was open for 3% of the time, Pallas kernels for 0%

profile of v1, /device:TPU:4, one launch (start us, length us, event | category | flops | bytes accessed | tf_op | source)
XLA Modules:
  0.0 180.8 jit_solution(8498864407674787726)
XLA Ops:
  7.3 2.6 %stack.2 = bf16[32,256,128]{2,1,0:T(8,128)(2,1)} broadcast(bf16[256,128]{1,0:T(8,128)(2,1)} %param.9), dimensions={1,2} | broadcast | bytes 2162688 | tf_op jit(solution)/shard_map/stack | solution.py:98
  9.9 10.3 %all-to-all-start = ((bf16[32,256,128]{2,1,0:T(8,128)(2,1)}), bf16[32,256,128]{2,1,0:T(8,128)(2,1)}, u32[]{:S(2)}, u32[]{:S(2)}) async-start(bf16[32,256,128]{2,1,0:T(8,128)(2,1)} %stack.2), calls=%async_computation | async-start | bytes 4194304 | tf_op jit(solution)/shard_map/all_to_all | solution.py:98
  22.5 24.1 %all-to-all-done = bf16[32,256,128]{2,1,0:T(8,128)(2,1)} async-done(((bf16[32,256,128]{2,1,0:T(8,128)(2,1)}), bf16[32,256,128]{2,1,0:T(8,128)(2,1)}, u32[]{:S(2)}, u32[]{:S(2)}) %all-to-all-start) | async-done | bytes 2097184 | tf_op jit(solution)/shard_map/all_to_all | solution.py:98
  46.6 32.2 %all-gather.2.cloned.1.call-done = bf16[8192,128]{1,0:T(8,128)(2,1)} async-done(((bf16[256,128]{1,0:T(8,128)(2,1)}), bf16[8192,128]{1,0:T(8,128)(2,1)}) %all-gather.2.cloned.1.call-update) | async-done | bytes 2097168 | tf_op jit(solution)/shard_map/all_gather | solution.py:100
  78.9 94.0 %while.15 = (s32[]{:T(128)}, f32[256,8]{0,1:T(8,128)S(1)}, f32[256,8]{0,1:T(8,128)S(1)}, f32[256,8,128]{2,0,1:T(8,128)S(1)}, s32[256]{0:T(256)S(1)}, /*index=5*/...) while((s32[]{:T(128)}, f32[256,8]{0,1:T(8,128)S(1)}, ...), condition=%wide.region_6.7_spmd.clone, body=%wide.region_0.6_spmd.clone.sunk | while | flops 551555840 | bytes 16135525 | solution.py:57
  81.7 5.4 %conditional.3 = ((f32[256,8]{0,1:T(8,128)S(1)}, f32[256,8]{0,1:T(8,128)S(1)}, f32[256,8,128]{2,0,1:T(8,128)S(1)})) conditional(s32[]{:T(128)} %convert_element_type.27, (f32[256,8]{0,1:T(8,128)S(1)}, f32[256,8]{0,1:T(8,128)S(1)}, f32[256,8,128]{2,0,1:T(8,128)S(1)}) %tuple.45, (pred[256,512]{0,1:T(8,128)(4,1)S(1)}, s32[]{:T(128)}, ...), branch_computations={%region_2.2_spmd, %region_3.5_spmd} | conditional | flops 551030784 | bytes 15990858 | solution.py:55
  84.5 2.6 %fusion.8 = f32[256,8,128]{2,0,1:T(8,128)S(1)} fusion(f32[512,256,8]{1,0,2:T(8,128)S(1)} %get-tuple-element.234, f32[256,8]{0,1:T(8,128)S(1)} %max.7, pred[256,512]{0,1:T(8,128)(4,1)S(1)} %get-tuple-element.142, f32[256,8,128]{2,0,1:T(8,128)S(1)} %get-tuple-element.147, f32[256,8]{0,1:T(8,128)S(1)} %get-tuple-element.230, ...), kind=kOutput, calls=%fused_computation.9 | convolution fusion | flops 274202624 | bytes 6569988 | tf_op jit(solution)/shard_map/while/body/eval_jaxpr/cond/branch_1_fun/ths,sd->thd/dot_general | solution.py:44
  89.9 5.4 %conditional.3 = ((f32[256,8]{0,1:T(8,128)S(1)}, f32[256,8]{0,1:T(8,128)S(1)}, f32[256,8,128]{2,0,1:T(8,128)S(1)})) conditional(s32[]{:T(128)} %convert_element_type.27, (f32[256,8]{0,1:T(8,128)S(1)}, f32[256,8]{0,1:T(8,128)S(1)}, f32[256,8,128]{2,0,1:T(8,128)S(1)}) %tuple.45, (pred[256,512]{0,1:T(8,128)(4,1)S(1)}, s32[]{:T(128)}, ...), branch_computations={%region_2.2_spmd, %region_3.5_spmd} | conditional | flops 551030784 | bytes 15990858 | solution.py:55
  92.7 2.6 %fusion.8 = f32[256,8,128]{2,0,1:T(8,128)S(1)} fusion(f32[512,256,8]{1,0,2:T(8,128)S(1)} %get-tuple-element.234, f32[256,8]{0,1:T(8,128)S(1)} %max.7, pred[256,512]{0,1:T(8,128)(4,1)S(1)} %get-tuple-element.142, f32[256,8,128]{2,0,1:T(8,128)S(1)} %get-tuple-element.147, f32[256,8]{0,1:T(8,128)S(1)} %get-tuple-element.230, ...), kind=kOutput, calls=%fused_computation.9 | convolution fusion | flops 274202624 | bytes 6569988 | tf_op jit(solution)/shard_map/while/body/eval_jaxpr/cond/branch_1_fun/ths,sd->thd/dot_general | solution.py:44
  98.1 5.4 %conditional.3 = ((f32[256,8]{0,1:T(8,128)S(1)}, f32[256,8]{0,1:T(8,128)S(1)}, f32[256,8,128]{2,0,1:T(8,128)S(1)})) conditional(s32[]{:T(128)} %convert_element_type.27, (f32[256,8]{0,1:T(8,128)S(1)}, f32[256,8]{0,1:T(8,128)S(1)}, f32[256,8,128]{2,0,1:T(8,128)S(1)}) %tuple.45, (pred[256,512]{0,1:T(8,128)(4,1)S(1)}, s32[]{:T(128)}, ...), branch_computations={%region_2.2_spmd, %region_3.5_spmd} | conditional | flops 551030784 | bytes 15990858 | solution.py:55
  100.9 2.6 %fusion.8 = f32[256,8,128]{2,0,1:T(8,128)S(1)} fusion(f32[512,256,8]{1,0,2:T(8,128)S(1)} %get-tuple-element.234, f32[256,8]{0,1:T(8,128)S(1)} %max.7, pred[256,512]{0,1:T(8,128)(4,1)S(1)} %get-tuple-element.142, f32[256,8,128]{2,0,1:T(8,128)S(1)} %get-tuple-element.147, f32[256,8]{0,1:T(8,128)S(1)} %get-tuple-element.230, ...), kind=kOutput, calls=%fused_computation.9 | convolution fusion | flops 274202624 | bytes 6569988 | tf_op jit(solution)/shard_map/while/body/eval_jaxpr/cond/branch_1_fun/ths,sd->thd/dot_general | solution.py:44
  106.4 5.4 %conditional.3 = ((f32[256,8]{0,1:T(8,128)S(1)}, f32[256,8]{0,1:T(8,128)S(1)}, f32[256,8,128]{2,0,1:T(8,128)S(1)})) conditional(s32[]{:T(128)} %convert_element_type.27, (f32[256,8]{0,1:T(8,128)S(1)}, f32[256,8]{0,1:T(8,128)S(1)}, f32[256,8,128]{2,0,1:T(8,128)S(1)}) %tuple.45, (pred[256,512]{0,1:T(8,128)(4,1)S(1)}, s32[]{:T(128)}, ...), branch_computations={%region_2.2_spmd, %region_3.5_spmd} | conditional | flops 551030784 | bytes 15990858 | solution.py:55
  109.2 2.6 %fusion.8 = f32[256,8,128]{2,0,1:T(8,128)S(1)} fusion(f32[512,256,8]{1,0,2:T(8,128)S(1)} %get-tuple-element.234, f32[256,8]{0,1:T(8,128)S(1)} %max.7, pred[256,512]{0,1:T(8,128)(4,1)S(1)} %get-tuple-element.142, f32[256,8,128]{2,0,1:T(8,128)S(1)} %get-tuple-element.147, f32[256,8]{0,1:T(8,128)S(1)} %get-tuple-element.230, ...), kind=kOutput, calls=%fused_computation.9 | convolution fusion | flops 274202624 | bytes 6569988 | tf_op jit(solution)/shard_map/while/body/eval_jaxpr/cond/branch_1_fun/ths,sd->thd/dot_general | solution.py:44
  114.6 5.4 %conditional.3 = ((f32[256,8]{0,1:T(8,128)S(1)}, f32[256,8]{0,1:T(8,128)S(1)}, f32[256,8,128]{2,0,1:T(8,128)S(1)})) conditional(s32[]{:T(128)} %convert_element_type.27, (f32[256,8]{0,1:T(8,128)S(1)}, f32[256,8]{0,1:T(8,128)S(1)}, f32[256,8,128]{2,0,1:T(8,128)S(1)}) %tuple.45, (pred[256,512]{0,1:T(8,128)(4,1)S(1)}, s32[]{:T(128)}, ...), branch_computations={%region_2.2_spmd, %region_3.5_spmd} | conditional | flops 551030784 | bytes 15990858 | solution.py:55
  114.6 1.7 fusion.2
  117.4 2.6 %fusion.8 = f32[256,8,128]{2,0,1:T(8,128)S(1)} fusion(f32[512,256,8]{1,0,2:T(8,128)S(1)} %get-tuple-element.234, f32[256,8]{0,1:T(8,128)S(1)} %max.7, pred[256,512]{0,1:T(8,128)(4,1)S(1)} %get-tuple-element.142, f32[256,8,128]{2,0,1:T(8,128)S(1)} %get-tuple-element.147, f32[256,8]{0,1:T(8,128)S(1)} %get-tuple-element.230, ...), kind=kOutput, calls=%fused_computation.9 | convolution fusion | flops 274202624 | bytes 6569988 | tf_op jit(solution)/shard_map/while/body/eval_jaxpr/cond/branch_1_fun/ths,sd->thd/dot_general | solution.py:44
  122.8 5.4 %conditional.3 = ((f32[256,8]{0,1:T(8,128)S(1)}, f32[256,8]{0,1:T(8,128)S(1)}, f32[256,8,128]{2,0,1:T(8,128)S(1)})) conditional(s32[]{:T(128)} %convert_element_type.27, (f32[256,8]{0,1:T(8,128)S(1)}, f32[256,8]{0,1:T(8,128)S(1)}, f32[256,8,128]{2,0,1:T(8,128)S(1)}) %tuple.45, (pred[256,512]{0,1:T(8,128)(4,1)S(1)}, s32[]{:T(128)}, ...), branch_computations={%region_2.2_spmd, %region_3.5_spmd} | conditional | flops 551030784 | bytes 15990858 | solution.py:55
  125.7 2.6 %fusion.8 = f32[256,8,128]{2,0,1:T(8,128)S(1)} fusion(f32[512,256,8]{1,0,2:T(8,128)S(1)} %get-tuple-element.234, f32[256,8]{0,1:T(8,128)S(1)} %max.7, pred[256,512]{0,1:T(8,128)(4,1)S(1)} %get-tuple-element.142, f32[256,8,128]{2,0,1:T(8,128)S(1)} %get-tuple-element.147, f32[256,8]{0,1:T(8,128)S(1)} %get-tuple-element.230, ...), kind=kOutput, calls=%fused_computation.9 | convolution fusion | flops 274202624 | bytes 6569988 | tf_op jit(solution)/shard_map/while/body/eval_jaxpr/cond/branch_1_fun/ths,sd->thd/dot_general | solution.py:44
  131.1 5.4 %conditional.3 = ((f32[256,8]{0,1:T(8,128)S(1)}, f32[256,8]{0,1:T(8,128)S(1)}, f32[256,8,128]{2,0,1:T(8,128)S(1)})) conditional(s32[]{:T(128)} %convert_element_type.27, (f32[256,8]{0,1:T(8,128)S(1)}, f32[256,8]{0,1:T(8,128)S(1)}, f32[256,8,128]{2,0,1:T(8,128)S(1)}) %tuple.45, (pred[256,512]{0,1:T(8,128)(4,1)S(1)}, s32[]{:T(128)}, ...), branch_computations={%region_2.2_spmd, %region_3.5_spmd} | conditional | flops 551030784 | bytes 15990858 | solution.py:55
  133.9 2.6 %fusion.8 = f32[256,8,128]{2,0,1:T(8,128)S(1)} fusion(f32[512,256,8]{1,0,2:T(8,128)S(1)} %get-tuple-element.234, f32[256,8]{0,1:T(8,128)S(1)} %max.7, pred[256,512]{0,1:T(8,128)(4,1)S(1)} %get-tuple-element.142, f32[256,8,128]{2,0,1:T(8,128)S(1)} %get-tuple-element.147, f32[256,8]{0,1:T(8,128)S(1)} %get-tuple-element.230, ...), kind=kOutput, calls=%fused_computation.9 | convolution fusion | flops 274202624 | bytes 6569988 | tf_op jit(solution)/shard_map/while/body/eval_jaxpr/cond/branch_1_fun/ths,sd->thd/dot_general | solution.py:44
  139.3 5.4 %conditional.3 = ((f32[256,8]{0,1:T(8,128)S(1)}, f32[256,8]{0,1:T(8,128)S(1)}, f32[256,8,128]{2,0,1:T(8,128)S(1)})) conditional(s32[]{:T(128)} %convert_element_type.27, (f32[256,8]{0,1:T(8,128)S(1)}, f32[256,8]{0,1:T(8,128)S(1)}, f32[256,8,128]{2,0,1:T(8,128)S(1)}) %tuple.45, (pred[256,512]{0,1:T(8,128)(4,1)S(1)}, s32[]{:T(128)}, ...), branch_computations={%region_2.2_spmd, %region_3.5_spmd} | conditional | flops 551030784 | bytes 15990858 | solution.py:55
  142.1 2.6 %fusion.8 = f32[256,8,128]{2,0,1:T(8,128)S(1)} fusion(f32[512,256,8]{1,0,2:T(8,128)S(1)} %get-tuple-element.234, f32[256,8]{0,1:T(8,128)S(1)} %max.7, pred[256,512]{0,1:T(8,128)(4,1)S(1)} %get-tuple-element.142, f32[256,8,128]{2,0,1:T(8,128)S(1)} %get-tuple-element.147, f32[256,8]{0,1:T(8,128)S(1)} %get-tuple-element.230, ...), kind=kOutput, calls=%fused_computation.9 | convolution fusion | flops 274202624 | bytes 6569988 | tf_op jit(solution)/shard_map/while/body/eval_jaxpr/cond/branch_1_fun/ths,sd->thd/dot_general | solution.py:44
  147.6 5.4 %conditional.3 = ((f32[256,8]{0,1:T(8,128)S(1)}, f32[256,8]{0,1:T(8,128)S(1)}, f32[256,8,128]{2,0,1:T(8,128)S(1)})) conditional(s32[]{:T(128)} %convert_element_type.27, (f32[256,8]{0,1:T(8,128)S(1)}, f32[256,8]{0,1:T(8,128)S(1)}, f32[256,8,128]{2,0,1:T(8,128)S(1)}) %tuple.45, (pred[256,512]{0,1:T(8,128)(4,1)S(1)}, s32[]{:T(128)}, ...), branch_computations={%region_2.2_spmd, %region_3.5_spmd} | conditional | flops 551030784 | bytes 15990858 | solution.py:55
  150.4 2.6 %fusion.8 = f32[256,8,128]{2,0,1:T(8,128)S(1)} fusion(f32[512,256,8]{1,0,2:T(8,128)S(1)} %get-tuple-element.234, f32[256,8]{0,1:T(8,128)S(1)} %max.7, pred[256,512]{0,1:T(8,128)(4,1)S(1)} %get-tuple-element.142, f32[256,8,128]{2,0,1:T(8,128)S(1)} %get-tuple-element.147, f32[256,8]{0,1:T(8,128)S(1)} %get-tuple-element.230, ...), kind=kOutput, calls=%fused_computation.9 | convolution fusion | flops 274202624 | bytes 6569988 | tf_op jit(solution)/shard_map/while/body/eval_jaxpr/cond/branch_1_fun/ths,sd->thd/dot_general | solution.py:44
  (148 shorter events, 52.1 us)
Async XLA Ops:
  6.5 13.7 %copy-start.1 = (bf16[256,1024]{1,0:T(8,128)(2,1)S(1)}, bf16[256,1024]{1,0:T(8,128)(2,1)}, u32[]{:S(2)}) copy-start(bf16[256,1024]{1,0:T(8,128)(2,1)} %param.8) | copy-start | bytes 1572868
  6.5 72.2 %all-gather.2.cloned.1.call-start = ((), (), s32[]{:S(2)}) async-start(), calls=%async_computation.1 | async-start | bytes 2162688 | tf_op jit(solution)/shard_map/all_gather | solution.py:100
  7.3 13.5 %copy-start = (s32[8192]{0:T(1024)S(1)}, s32[8192]{0:T(1024)}, u32[]{:S(2)}) copy-start(s32[8192]{0:T(1024)} %param.11) | copy-start | bytes 98308
  9.9 36.7 %all-to-all-start = ((bf16[32,256,128]{2,1,0:T(8,128)(2,1)}), bf16[32,256,128]{2,1,0:T(8,128)(2,1)}, u32[]{:S(2)}, u32[]{:S(2)}) async-start(bf16[32,256,128]{2,1,0:T(8,128)(2,1)} %stack.2), calls=%async_computation | async-start | bytes 4194304 | tf_op jit(solution)/shard_map/all_to_all | solution.py:98
Sparse Core Ops, SparseCore 0:
  10.5 68.2 all-gather.1
